TPU v7x, 256 devices: a whole 4x4x8 slice. The times are simulated.
256 devices in a mesh: dp: 16 (over x, y_hi, core), expert: 16 (over z, y_lo).
Axes of the slice: x: 4, y: 4 (y_hi: 2, y_lo: 2; y = y_hi * 2 + y_lo), z: 8, core: 2. Of those that a mesh axis runs over, the one named last changes fastest.
Arguments:
- tokens: bfloat16 [2048, 4096], P('expert', 'dp'), may hold values from -6 to 6
- expert_ids: int32 [2048, 8], P('expert'), may hold values from 0 to 63, all different within a row; in each aligned block of 128 rows (0 to 127, 128 to 255, ...) at most 32 rows name the same one
- gate_prob: float32 [2048, 8], P('expert'), may hold values from 0.05 to 0.35
- w_gate: bfloat16 [64, 4096, 768], P('expert', 'dp'), may hold values from -0.09375 to 0.09375
- w_up: bfloat16 [64, 4096, 768], P('expert', 'dp'), may hold values from -0.09375 to 0.09375
- w_down: bfloat16 [64, 768, 4096], P('expert', None, 'dp'), may hold values from -0.21875 to 0.21875
- grad_out: bfloat16 [2048, 4096], P('expert', 'dp'), may hold values from -6 to 6
Outputs:
- mixed: bfloat16 [2048, 4096], P('expert', 'dp')
- grad_tokens: bfloat16 [2048, 4096], P('expert', 'dp')
- grad_gate: float32 [2048, 8], P('expert')
- grad_w_gate: bfloat16 [64, 4096, 768], P('expert', 'dp')
- grad_w_up: bfloat16 [64, 4096, 768], P('expert', 'dp')
- grad_w_down: bfloat16 [64, 768, 4096], P('expert', None, 'dp')
Inputs may be any that keep to these rules, and one draw needn't show every extreme that they name: `expert_ids`: each row names 8 different experts. Within the rows of one index of expert (aligned blocks of 128 rows) no expert is named by more than 32 rows, a bound that some block reaches.
All inputs are finite; a program needn't handle non-finite values.
Results may differ from a plain program's by a relative error of at most 0.035.
Values may be sent and summed in bfloat16 or wider, within the bound.
No kernel may reach another device: no remote copies, remote signals or barrier semaphores. Data moves between devices by JAX's collectives and lax.ppermute only.
A program may use at most 128 MiB of HBM per device.

v0:
```python
import jax
import jax.numpy as jnp
from jax import lax
from jax.sharding import PartitionSpec as P


def slot_tables(expert_ids, columns, per_device, capacity):
    flat_ids = expert_ids.reshape(-1)
    assign_count = flat_ids.shape[0]
    experts_all = columns * per_device
    onehot = (flat_ids[:, None] == jnp.arange(experts_all, dtype=jnp.int32)[None, :]).astype(
        jnp.int32
    )
    before = jnp.cumsum(onehot, axis=0) - onehot
    rank_in = jnp.sum(before * onehot, axis=1)
    slot_of = (flat_ids % per_device * columns + flat_ids // per_device) * capacity + rank_in
    slot_count = experts_all * capacity
    source = (
        jnp.full((slot_count,), assign_count, jnp.int32)
        .at[slot_of]
        .set(jnp.arange(assign_count, dtype=jnp.int32))
    )
    return (slot_of, source)


def run_groups(bundles, hidden_units):
    parties = lax.axis_size("dp")
    row_totals = [bundle[0].shape[0] * bundle[0].shape[1] for bundle in bundles]
    gate_part = jnp.concatenate(
        [
            jnp.einsum(
                "grd,gdf->grf", bundle[0], bundle[2], preferred_element_type=jnp.float32
            ).reshape(-1, hidden_units)
            for bundle in bundles
        ],
        axis=0,
    )
    up_part = jnp.concatenate(
        [
            jnp.einsum(
                "grd,gdf->grf", bundle[0], bundle[3], preferred_element_type=jnp.float32
            ).reshape(-1, hidden_units)
            for bundle in bundles
        ],
        axis=0,
    )
    total_rows = gate_part.shape[0]
    share_rows = total_rows // parties
    share_start = lax.axis_index("dp") * share_rows
    gate_pre, up_pre = (
        lax.psum(gate_part.astype(jnp.bfloat16), "dp").astype(jnp.float32),
        lax.psum(up_part.astype(jnp.bfloat16), "dp").astype(jnp.float32),
    )
    hidden = (jax.nn.silu(gate_pre) * up_pre).astype(jnp.bfloat16)
    gate_share = lax.dynamic_slice_in_dim(gate_pre, share_start, share_rows, 0)
    up_share = lax.dynamic_slice_in_dim(up_pre, share_start, share_rows, 0)
    hidden_part = jnp.concatenate(
        [
            jnp.einsum(
                "grd,gfd->grf", bundle[1], bundle[4], preferred_element_type=jnp.float32
            ).reshape(-1, hidden_units)
            for bundle in bundles
        ],
        axis=0,
    )
    hidden_grad = lax.psum_scatter(
        hidden_part.astype(jnp.bfloat16), "dp", scatter_dimension=0, tiled=True
    ).astype(jnp.float32)
    sigmoid_g = jax.nn.sigmoid(gate_share)
    gate_grad = (
        hidden_grad * up_share * sigmoid_g * (1.0 + gate_share * (1.0 - sigmoid_g))
    ).astype(jnp.bfloat16)
    up_grad = (hidden_grad * gate_share * sigmoid_g).astype(jnp.bfloat16)
    gate_rows, up_rows = (
        lax.all_gather(gate_grad, "dp", axis=0, tiled=True),
        lax.all_gather(up_grad, "dp", axis=0, tiled=True),
    )
    outputs = []
    offset = 0
    for bundle, row_total in zip(bundles, row_totals):
        piece_shape = (bundle[0].shape[0], bundle[0].shape[1], hidden_units)
        hidden_piece = hidden.reshape(piece_shape)
        gate_piece = gate_rows.reshape(piece_shape)
        up_piece = up_rows.reshape(piece_shape)
        offset = offset + row_total
        expert_out = jnp.einsum(
            "grf,gfd->grd", hidden_piece, bundle[4], preferred_element_type=jnp.float32
        ).astype(jnp.bfloat16)
        slot_grad = (
            jnp.einsum("grf,gdf->grd", gate_piece, bundle[2], preferred_element_type=jnp.float32)
            + jnp.einsum("grf,gdf->grd", up_piece, bundle[3], preferred_element_type=jnp.float32)
        ).astype(jnp.bfloat16)
        dw_gate = jnp.einsum(
            "grd,grf->gdf", bundle[0], gate_piece, preferred_element_type=jnp.float32
        )
        dw_up = jnp.einsum("grd,grf->gdf", bundle[0], up_piece, preferred_element_type=jnp.float32)
        dw_down = jnp.einsum(
            "grf,grd->gfd", hidden_piece, bundle[1], preferred_element_type=jnp.float32
        )
        outputs.append((expert_out, slot_grad, dw_gate, dw_up, dw_down))
    return outputs


def on_device(tokens, expert_ids, gate_prob, w_gate, w_up, w_down, grad_out):
    tok_rows, fanout = expert_ids.shape
    per_device, slice_width, hidden_units = w_gate.shape
    columns = lax.axis_size("expert")
    capacity = 2 * tok_rows * fanout // (per_device * columns)
    slot_count = per_device * columns * capacity
    assign_count = tok_rows * fanout
    slot_of, source = slot_tables(expert_ids, columns, per_device, capacity)
    filled = source < assign_count
    safe_src = jnp.minimum(source, assign_count - 1)
    tok_index = safe_src // fanout
    gate_flat = gate_prob.reshape(-1)
    token_buffer = jnp.where(filled[:, None], tokens[tok_index], jnp.zeros((), jnp.bfloat16))
    gate_slots = jnp.where(filled, gate_flat[safe_src], jnp.zeros((), jnp.float32))
    grad_buffer = (gate_slots[:, None] * grad_out[tok_index].astype(jnp.float32)).astype(
        jnp.bfloat16
    )
    layout = (per_device, columns, capacity, slice_width)
    sent_tokens, sent_grads = (
        lax.all_to_all(
            token_buffer.reshape(layout), "expert", split_axis=1, concat_axis=1, tiled=True
        ),
        lax.all_to_all(
            grad_buffer.reshape(layout), "expert", split_axis=1, concat_axis=1, tiled=True
        ),
    )
    bundles = [
        (
            sent_tokens.reshape(per_device, columns * capacity, slice_width),
            sent_grads.reshape(per_device, columns * capacity, slice_width),
            w_gate,
            w_up,
            w_down,
        )
    ]
    results = run_groups(bundles, hidden_units)
    expert_out = results[0][0].reshape(layout)
    slot_grad = results[0][1].reshape(layout)
    total_gate = results[0][2]
    total_up = results[0][3]
    total_down = results[0][4]
    grad_w_gate = total_gate.astype(jnp.bfloat16)
    grad_w_up = total_up.astype(jnp.bfloat16)
    grad_w_down = total_down.astype(jnp.bfloat16)
    back_out, back_grad = (
        lax.all_to_all(expert_out, "expert", split_axis=1, concat_axis=1, tiled=True),
        lax.all_to_all(slot_grad, "expert", split_axis=1, concat_axis=1, tiled=True),
    )
    out_rows = (
        back_out.reshape(slot_count, slice_width)[slot_of]
        .reshape(tok_rows, fanout, slice_width)
        .astype(jnp.float32)
    )
    grad_rows = (
        back_grad.reshape(slot_count, slice_width)[slot_of]
        .reshape(tok_rows, fanout, slice_width)
        .astype(jnp.float32)
    )
    mixed = jnp.sum(gate_prob[:, :, None] * out_rows, axis=1).astype(jnp.bfloat16)
    grad_tokens = jnp.sum(grad_rows, axis=1).astype(jnp.bfloat16)
    partial_dots = jnp.sum(out_rows * grad_out.astype(jnp.float32)[:, None, :], axis=2)
    grad_gate = lax.psum(partial_dots, "dp")
    return (mixed, grad_tokens, grad_gate, grad_w_gate, grad_w_up, grad_w_down)


def solution(mesh):
    return jax.shard_map(
        on_device,
        mesh=mesh,
        in_specs=(
            P("expert", "dp"),
            P("expert", None),
            P("expert", None),
            P("expert", "dp", None),
            P("expert", "dp", None),
            P("expert", None, "dp"),
            P("expert", "dp"),
        ),
        out_specs=(
            P("expert", "dp"),
            P("expert", "dp"),
            P("expert", None),
            P("expert", "dp", None),
            P("expert", "dp", None),
            P("expert", None, "dp"),
        ),
        check_vma=False,
    )
```

profile of v0, /device:TPU:32, one launch (start us, length us, event | category | flops | bytes accessed | tf_op | source)
XLA Modules:
  0.0 592.9 jit_solution(16468973395299543634)
XLA Ops:
  7.2 0.9 copy.47
  8.3 0.1 reshape.224
  8.4 0.8 copy.46
  9.2 0.1 reshape.230
  9.3 18.0 %reduce-window.6 = s32[64,8,128]{2,1,0:T(8,128)S(1)} reduce-window(s32[64,8,128]{2,1,0:T(8,128)S(1)} %fusion.11, s32[]{:T(128)} %constant.58.clone.1), window={size=1x1x128 pad=0_0x0_0x127_0}, to_apply=%region_0.0 | reduce-window | flops 8323072 | bytes 524292 | tf_op jit(solution)/shard_map/reduce-window
  27.3 0.1 slice.18
  27.5 0.1 copy.50
  27.7 0.1 broadcast_add_fusion
  28.0 4.3 scatter_custom_fusion
  32.4 8.6 %gather_fusion.2 = f32[2048]{0:T(1024)S(1)} fusion(f32[1024]{0:T(1024)S(1)} %reshape.230, s32[2048]{0:T(1024)S(1)} %get-tuple-element.26), kind=kCustom, calls=%fused_computation.2 | custom fusion | bytes 24576 | tf_op jit(solution)/shard_map/gather | solution.py:117
  41.1 7.5 %gather_fusion = bf16[2048,256]{1,0:T(8,128)(2,1)S(1)} fusion(bf16[128,256]{1,0:T(8,128)(2,1)S(1)} %copy-done.2, s32[2048]{0:T(1024)S(1)} %get-tuple-element.27), kind=kCustom, calls=%fused_computation | custom fusion | bytes 2105344 | tf_op jit(solution)/shard_map/gather | solution.py:116
  48.6 0.4 copy_select_fusion
  49.1 35.7 %all_to_all.20 = bf16[4,16,32,256]{3,2,0,1:T(8,128)(2,1)S(1)} all-to-all(bf16[4,16,32,256]{3,2,0,1:T(8,128)(2,1)S(1)} %copy_select_fusion), channel_id=1, replica_groups=mesh['dp'=16,'expert'=16] {'expert'}, dimensions={1} | all-to-all | bytes 2097152 | tf_op jit(solution)/shard_map/all_to_all | solution.py:123
  84.9 2.6 convolution_convert_fusion.1
  87.5 2.6 convolution_convert_fusion.2
  90.3 0.7 copy-done.1
  91.0 7.5 %gather_fusion.3 = bf16[2048,256]{1,0:T(8,128)(2,1)S(1)} fusion(bf16[128,256]{1,0:T(8,128)(2,1)S(1)} %copy-done.1, s32[2048]{0:T(1024)S(1)} %get-tuple-element.27), kind=kCustom, calls=%fused_computation.3 | custom fusion | bytes 2105344 | tf_op jit(solution)/shard_map/gather | solution.py:118
  98.5 0.3 fusion
  98.8 32.5 %all_to_all.21 = bf16[4,16,32,256]{3,2,0,1:T(8,128)(2,1)S(1)} all-to-all(bf16[4,16,32,256]{3,2,0,1:T(8,128)(2,1)S(1)} %fusion), channel_id=1, replica_groups=mesh['dp'=16,'expert'=16] {'expert'}, dimensions={1} | all-to-all | bytes 2097152 | tf_op jit(solution)/shard_map/all_to_all | solution.py:126
  131.4 2.7 convolution_convert_fusion
  134.2 139.9 %all-reduce.3.cloned.1.call-done = (bf16[2048,768]{1,0:T(8,128)(2,1)}, bf16[2048,768]{1,0:T(8,128)(2,1)}) async-done(((bf16[2048,768]{1,0:T(8,128)(2,1)}, bf16[2048,768]{1,0:T(8,128)(2,1)}), (bf16[2048,768]{1,0:T(8,128)(2,1)}, bf16[2048,768]{1,0:T(8,128)(2,1)})) %all-reduce.3.cloned.1.call-update) | async-done | bytes 6291472 | tf_op jit(solution)/shard_map/psum | solution.py:52
  274.1 5.2 convert_element_type.91
  279.3 3.1 convert_element_type.94
  282.4 79.0 %reduce-scatter.2.cloned.1.call-done = bf16[128,768]{1,0:T(8,128)(2,1)} async-done(((bf16[2048,768]{1,0:T(8,128)(2,1)}), bf16[128,768]{1,0:T(8,128)(2,1)}) %reduce-scatter.2.cloned.1.call-update) | async-done | bytes 196624 | tf_op jit(solution)/shard_map/reduce_scatter | solution.py:66
  361.5 2.1 fusion.7
  363.7 0.5 all-gather.5.cloned.1.call-update
  364.2 3.8 multiply_convert_fusion
  368.1 1.0 convolution_convert_fusion.6
  369.1 0.7 copy-done.7
  369.8 1.0 copy.55
  370.8 7.5 %all-to-all-start.1 = ((bf16[4,16,32,256]{3,2,0,1:T(8,128)(2,1)}), bf16[4,16,32,256]{3,2,0,1:T(8,128)(2,1)}, u32[]{:S(2)}, u32[]{:S(2)}) async-start(bf16[4,16,32,256]{3,2,0,1:T(8,128)(2,1)} %copy.55), calls=%async_computation.1 | async-start | bytes 2097152 | tf_op jit(solution)/shard_map/all_to_all | solution.py:149
  378.3 42.8 %all-gather.3.cloned.1.call-done = bf16[2048,768]{1,0:T(8,128)(2,1)} async-done(((bf16[128,768]{1,0:T(8,128)(2,1)}), bf16[2048,768]{1,0:T(8,128)(2,1)}) %all-gather.3.cloned.1.call-update) | async-done | bytes 3145744 | tf_op jit(solution)/shard_map/all_gather | solution.py:75
  421.1 4.7 fusion.20
  425.8 54.7 %all-gather.5.cloned.1.call-done = bf16[2048,768]{1,0:T(8,128)(2,1)} async-done(((bf16[128,768]{1,0:T(8,128)(2,1)}), bf16[2048,768]{1,0:T(8,128)(2,1)}) %all-gather.5.cloned.1.call-update) | async-done | bytes 3145744 | tf_op jit(solution)/shard_map/all_gather | solution.py:76
  480.5 4.0 add_convert_fusion
  484.5 1.1 copy.61
  485.6 7.5 %all-to-all-start.3 = ((bf16[4,16,32,256]{3,2,0,1:T(8,128)(2,1)}), bf16[4,16,32,256]{3,2,0,1:T(8,128)(2,1)}, u32[]{:S(2)}, u32[]{:S(2)}) async-start(bf16[4,16,32,256]{3,2,0,1:T(8,128)(2,1)} %copy.61), calls=%async_computation.4 | async-start | bytes 2097152 | tf_op jit(solution)/shard_map/all_to_all | solution.py:150
  493.1 4.3 convolution_convert_fusion.3
  497.4 1.3 copy.56
  498.7 3.9 gather_fusion.1
  502.7 1.1 fusion.2
  503.8 69.0 %psum.23 = f32[128,8]{1,0:T(8,128)S(1)} all-reduce(f32[128,8]{1,0:T(8,128)S(1)} %get-tuple-element.18), channel_id=1, replica_groups=mesh['dp'=16,'expert'=16] {'dp'}, use_global_device_ids=true, to_apply=%region_10.11 | all-reduce | flops 1024 | bytes 8192 | tf_op jit(solution)/shard_map/psum | solution.py:165
  572.8 0.7 copy.66
  573.4 4.5 convolution_convert_fusion.5
  578.0 2.2 convolution_convert_fusion.4
  580.2 1.3 copy.62
  581.5 3.9 gather_fusion.4
  585.4 1.0 bitcast_reduce_fusion
  (46 shorter events, 1.1 us)
Async XLA Ops:
  7.2 124.3 %copy-start = (bf16[4,768,256]{2,1,0:T(8,128)(2,1)S(1)}, bf16[4,768,256]{2,1,0:T(8,128)(2,1)}, u32[]{:S(2)}) copy-start(bf16[4,768,256]{2,1,0:T(8,128)(2,1)} %param.12) | copy-start | bytes 4718596
  7.2 266.9 %all-reduce.3.cloned.1.call-start = ((), (), s32[]{:S(2)}) async-start(), calls=%async_computation.8 | async-start | bytes 12582912 | tf_op jit(solution)/shard_map/psum | solution.py:52
  32.4 8.7 %copy-start.2 = (bf16[128,256]{1,0:T(8,128)(2,1)S(1)}, bf16[128,256]{1,0:T(8,128)(2,1)}, u32[]{:S(2)}) copy-start(bf16[128,256]{1,0:T(8,128)(2,1)} %param.7) | copy-start | bytes 196612
  48.6 36.3 %copy-start.9 = (bf16[4,256,768]{2,1,0:T(8,128)(2,1)S(1)}, bf16[4,256,768]{2,1,0:T(8,128)(2,1)}, u32[]{:S(2)}) copy-start(bf16[4,256,768]{2,1,0:T(8,128)(2,1)} %param.11) | copy-start | bytes 4718596
  84.8 5.3 copy-start.3
  84.8 2.7 copy-start.8
  90.2 0.8 copy-start.1
  90.2 271.3 %reduce-scatter.2.cloned.1.call-start = ((), (), s32[]{:S(2)}) async-start(), calls=%async_computation.5 | async-start | bytes 3342336 | tf_op jit(solution)/shard_map/reduce_scatter | solution.py:66
  134.2 287.0 %all-gather.3.cloned.1.call-start = ((), (), s32[]{:S(2)}) async-start(), calls=%async_computation.6 | async-start | bytes 3342336 | tf_op jit(solution)/shard_map/all_gather | solution.py:75
  274.1 5.2 copy-start.5
  363.6 116.8 %all-gather.5.cloned.1.call-start = ((), (), s32[]{:S(2)}) async-start(), calls=%async_computation.7 | async-start | bytes 3342336 | tf_op jit(solution)/shard_map/all_gather | solution.py:76
  368.1 1.7 copy-start.7
  370.8 114.8 %all-to-all-start.1 = ((bf16[4,16,32,256]{3,2,0,1:T(8,128)(2,1)}), bf16[4,16,32,256]{3,2,0,1:T(8,128)(2,1)}, u32[]{:S(2)}, u32[]{:S(2)}) async-start(bf16[4,16,32,256]{3,2,0,1:T(8,128)(2,1)} %copy.55), calls=%async_computation.1 | async-start | bytes 2097152 | tf_op jit(solution)/shard_map/all_to_all | solution.py:149
  485.6 94.6 %all-to-all-start.3 = ((bf16[4,16,32,256]{3,2,0,1:T(8,128)(2,1)}), bf16[4,16,32,256]{3,2,0,1:T(8,128)(2,1)}, u32[]{:S(2)}, u32[]{:S(2)}) async-start(bf16[4,16,32,256]{3,2,0,1:T(8,128)(2,1)} %copy.61), calls=%async_computation.4 | async-start | bytes 2097152 | tf_op jit(solution)/shard_map/all_to_all | solution.py:150
  503.8 74.2 %copy-start.4 = (bf16[4,16,32,256]{3,2,1,0:T(8,128)(2,1)S(1)}, bf16[4,16,32,256]{3,2,1,0:T(8,128)(2,1)}, u32[]{:S(2)}) copy-start(bf16[4,16,32,256]{3,2,1,0:T(8,128)(2,1)} %copy-done.3) | copy-start | bytes 3145732
  573.4 4.5 copy-start.6
Sparse Core Ops, SparseCore 0:
  90.3 183.7 all-reduce.2
  278.4 83.0 reduce-scatter.1
  364.2 56.9 all-gather.2
  424.2 56.2 all-gather.4
where the time goes:
time: 594 us; the launch traced here: 593 us
  waiting for transfers between devices  317 us (53%)
  blocking collectives  137 us (23%)
  local copies, waits for them, and re-layouts  45.3 us (8%)
  other arithmetic  35.5 us (6%)
  matrix products  28.7 us (5%)
  starting transfers between devices  15.2 us (3%)
  between operations  14.1 us (2%)
    psum x1, waiting for transfers between devices, run_groups(): lax.psum(up_part.astype(jnp.bfloat16), 'dp').astype(jnp.float32)  140 us
    reduce_scatter x1, waiting for transfers between devices, run_groups(): lax.psum_scatter(hidden_part.astype(jnp.bfloat16), 'dp', scatter_dimensio...  79 us
    psum x1, blocking collectives, on_device(): grad_gate = lax.psum(partial_dots, 'dp')  69 us
    all_gather x1, waiting for transfers between devices, run_groups(): lax.all_gather(up_grad, 'dp', axis=0, tiled=True)  54.7 us
    all_gather x1, waiting for transfers between devices, run_groups(): lax.all_gather(gate_grad, 'dp', axis=0, tiled=True)  42.8 us
    all_to_all x1, blocking collectives, on_device(): lax.all_to_all(token_buffer.reshape(layout), 'expert', split_axis=1, conc...  35.7 us
    all_to_all x1, blocking collectives, on_device(): lax.all_to_all(grad_buffer.reshape(layout), 'expert', split_axis=1, conca...  32.5 us
    another operation x3, other arithmetic  18.2 us
  transfers between devices with their start and end apart: 6, of which 4 were waited for; matrix products, arithmetic and copies ran while one was open for 9% of the time, Pallas kernels for 0%

commit v1 on v0

--- a/solution.py
+++ b/solution.py
@@ -1,7 +1,24 @@
+import functools
 import jax
 import jax.numpy as jnp
 from jax import lax
 from jax.sharding import PartitionSpec as P
+
+
+def balance_sides(array_in, array_axis, row_axis):
+    next_value = jnp.concatenate(
+        lax.all_to_all(
+            jnp.stack(lax.axis_size(row_axis) * [array_in]),
+            axis_name=row_axis,
+            split_axis=0,
+            concat_axis=0,
+        ),
+        axis=array_axis,
+    )
+    return next_value
+
+
+wrap_the_cards = functools.partial(balance_sides, array_axis=0, row_axis="dp")
 
 
 def slot_tables(expert_ids, columns, per_device, capacity):
@@ -73,7 +90,7 @@
     up_grad = (hidden_grad * gate_share * sigmoid_g).astype(jnp.bfloat16)
     gate_rows, up_rows = (
         lax.all_gather(gate_grad, "dp", axis=0, tiled=True),
-        lax.all_gather(up_grad, "dp", axis=0, tiled=True),
+        wrap_the_cards(up_grad),
     )
     outputs = []
     offset = 0

time: 594 us -> 561 us (0.944)
  waiting for transfers between devices: 317 us -> 280 us
  starting transfers between devices: 15.2 us -> 21.7 us
    all_gather x1 -> x0, waiting for transfers between devices: 54.7 us -> none  [run_groups(): lax.all_gather(up_grad, 'dp', axis=0, tiled=True)]
    all_to_all x0 -> x1, waiting for transfers between devices: none -> 37.1 us  [balance_sides(): lax.all_to_all(jnp.stack(lax.axis_size(row_axis) * [array_in]), axis_name...]
    all_gather x1, waiting for transfers between devices: 42.8 us -> 23.2 us  [run_groups(): lax.all_gather(gate_grad, 'dp', axis=0, tiled=True)]
where the time goes in v1:
time: 561 us
  waiting for transfers between devices  280 us (50%)
  blocking collectives  136 us (24%)
  local copies, waits for them, and re-layouts  47.3 us (8%)
  other arithmetic  35.4 us (6%)
  matrix products  26.3 us (5%)
  starting transfers between devices  21.7 us (4%)
  between operations  14.1 us (3%)
    psum x1, waiting for transfers between devices, run_groups(): lax.psum(up_part.astype(jnp.bfloat16), 'dp').astype(jnp.float32)  141 us
    reduce_scatter x1, waiting for transfers between devices, run_groups(): lax.psum_scatter(hidden_part.astype(jnp.bfloat16), 'dp', scatter_dimensio...  79 us
    psum x1, blocking collectives, on_device(): grad_gate = lax.psum(partial_dots, 'dp')  67.8 us
    all_to_all x1, waiting for transfers between devices, balance_sides(): lax.all_to_all(jnp.stack(lax.axis_size(row_axis) * [array_in]), axis_name...  37.1 us
    all_to_all x1, blocking collectives, on_device(): lax.all_to_all(token_buffer.reshape(layout), 'expert', split_axis=1, conc...  35.7 us
    all_to_all x1, blocking collectives, on_device(): lax.all_to_all(grad_buffer.reshape(layout), 'expert', split_axis=1, conca...  32.5 us
    all_gather x1, waiting for transfers between devices, run_groups(): lax.all_gather(gate_grad, 'dp', axis=0, tiled=True)  23.2 us
    another operation x3, other arithmetic  18.2 us
  transfers between devices with their start and end apart: 6, of which 4 were waited for; matrix products, arithmetic and copies ran while one was open for 9% of the time, Pallas kernels for 0%

profile of v1, /device:TPU:32, one launch (start us, length us, event | category | flops | bytes accessed | tf_op | source)
XLA Modules:
  0.0 560.7 jit_solution(265368643715612180)
XLA Ops:
  7.2 0.9 copy.47
  8.3 0.1 reshape.223
  8.4 0.8 copy.46
  9.3 18.0 %reduce-window.6 = s32[64,8,128]{2,1,0:T(8,128)S(1)} reduce-window(s32[64,8,128]{2,1,0:T(8,128)S(1)} %fusion.11, s32[]{:T(128)} %constant.58.clone.1), window={size=1x1x128 pad=0_0x0_0x127_0}, to_apply=%region_0.0 | reduce-window | flops 8323072 | bytes 524292 | tf_op jit(solution)/shard_map/reduce-window
  27.3 0.1 slice.18
  27.5 0.1 copy.50
  27.7 0.1 broadcast_add_fusion
  28.0 4.3 scatter_custom_fusion
  32.4 8.6 %gather_fusion.2 = f32[2048]{0:T(1024)S(1)} fusion(f32[1024]{0:T(1024)S(1)} %reshape.229, s32[2048]{0:T(1024)S(1)} %get-tuple-element.26), kind=kCustom, calls=%fused_computation.2 | custom fusion | bytes 24576 | tf_op jit(solution)/shard_map/gather | solution.py:134
  41.1 7.5 %gather_fusion = bf16[2048,256]{1,0:T(8,128)(2,1)S(1)} fusion(bf16[128,256]{1,0:T(8,128)(2,1)S(1)} %copy-done.2, s32[2048]{0:T(1024)S(1)} %get-tuple-element.27), kind=kCustom, calls=%fused_computation | custom fusion | bytes 2105344 | tf_op jit(solution)/shard_map/gather | solution.py:133
  48.6 0.4 copy_select_fusion
  49.1 35.7 %all_to_all.25 = bf16[4,16,32,256]{3,2,0,1:T(8,128)(2,1)S(1)} all-to-all(bf16[4,16,32,256]{3,2,0,1:T(8,128)(2,1)S(1)} %copy_select_fusion), channel_id=1, replica_groups=mesh['dp'=16,'expert'=16] {'expert'}, dimensions={1} | all-to-all | bytes 2097152 | tf_op jit(solution)/shard_map/all_to_all | solution.py:140
  84.9 2.6 convolution_convert_fusion.1
  87.5 2.6 convolution_convert_fusion.2
  90.3 0.7 copy-done.1
  91.0 7.5 %gather_fusion.3 = bf16[2048,256]{1,0:T(8,128)(2,1)S(1)} fusion(bf16[128,256]{1,0:T(8,128)(2,1)S(1)} %copy-done.1, s32[2048]{0:T(1024)S(1)} %get-tuple-element.27), kind=kCustom, calls=%fused_computation.3 | custom fusion | bytes 2105344 | tf_op jit(solution)/shard_map/gather | solution.py:135
  98.5 0.3 fusion
  98.8 32.5 %all_to_all.26 = bf16[4,16,32,256]{3,2,0,1:T(8,128)(2,1)S(1)} all-to-all(bf16[4,16,32,256]{3,2,0,1:T(8,128)(2,1)S(1)} %fusion), channel_id=1, replica_groups=mesh['dp'=16,'expert'=16] {'expert'}, dimensions={1} | all-to-all | bytes 2097152 | tf_op jit(solution)/shard_map/all_to_all | solution.py:143
  131.4 2.7 convolution_convert_fusion
  134.2 140.5 %all-reduce.3.cloned.1.call-done = (bf16[2048,768]{1,0:T(8,128)(2,1)}, bf16[2048,768]{1,0:T(8,128)(2,1)}) async-done(((bf16[2048,768]{1,0:T(8,128)(2,1)}, bf16[2048,768]{1,0:T(8,128)(2,1)}), (bf16[2048,768]{1,0:T(8,128)(2,1)}, bf16[2048,768]{1,0:T(8,128)(2,1)})) %all-reduce.3.cloned.1.call-update) | async-done | bytes 6291472 | tf_op jit(solution)/shard_map/psum | solution.py:69
  274.8 5.2 convert_element_type.91
  279.9 3.1 convert_element_type.94
  283.1 79.0 %reduce-scatter.2.cloned.1.call-done = bf16[128,768]{1,0:T(8,128)(2,1)} async-done(((bf16[2048,768]{1,0:T(8,128)(2,1)}), bf16[128,768]{1,0:T(8,128)(2,1)}) %reduce-scatter.2.cloned.1.call-update) | async-done | bytes 196624 | tf_op jit(solution)/shard_map/reduce_scatter | solution.py:83
  362.1 2.1 fusion.7
  364.2 2.0 stack.2
  366.2 4.5 all-to-all-start.3
  370.7 3.8 multiply_convert_fusion
  374.6 1.0 convolution_convert_fusion.6
  375.5 0.6 copy-done.7
  376.2 1.0 copy.55
  377.2 37.1 %all-to-all-done.3 = bf16[16,128,768]{2,1,0:T(8,128)(2,1)} async-done(((bf16[16,128,768]{2,1,0:T(8,128)(2,1)}), bf16[16,128,768]{2,1,0:T(8,128)(2,1)}, u32[]{:S(2)}, u32[]{:S(2)}) %all-to-all-start.3) | async-done | bytes 3145760 | tf_op jit(solution)/shard_map/all_to_all | solution.py:10
  414.3 7.8 %all-to-all-start.1 = ((bf16[4,16,32,256]{3,2,0,1:T(8,128)(2,1)}), bf16[4,16,32,256]{3,2,0,1:T(8,128)(2,1)}, u32[]{:S(2)}, u32[]{:S(2)}) async-start(bf16[4,16,32,256]{3,2,0,1:T(8,128)(2,1)} %copy.55), calls=%async_computation.1 | async-start | bytes 2097152 | tf_op jit(solution)/shard_map/all_to_all | solution.py:166
  422.1 23.2 %all-gather.2.cloned.1.call-done = bf16[2048,768]{1,0:T(8,128)(2,1)} async-done(((bf16[128,768]{1,0:T(8,128)(2,1)}), bf16[2048,768]{1,0:T(8,128)(2,1)}) %all-gather.2.cloned.1.call-update) | async-done | bytes 3145744 | tf_op jit(solution)/shard_map/all_gather | solution.py:92
  445.3 3.5 fusion.20
  448.8 2.9 add_convert_fusion
  451.7 1.1 copy.61
  452.8 9.2 %all-to-all-start.4 = ((bf16[4,16,32,256]{3,2,0,1:T(8,128)(2,1)}), bf16[4,16,32,256]{3,2,0,1:T(8,128)(2,1)}, u32[]{:S(2)}, u32[]{:S(2)}) async-start(bf16[4,16,32,256]{3,2,0,1:T(8,128)(2,1)} %copy.61), calls=%async_computation.5 | async-start | bytes 2097152 | tf_op jit(solution)/shard_map/all_to_all | solution.py:167
  462.1 4.3 convolution_convert_fusion.3
  466.4 1.3 copy.56
  467.7 3.9 gather_fusion.1
  471.6 1.1 fusion.2
  472.8 67.8 %psum.23 = f32[128,8]{1,0:T(8,128)S(1)} all-reduce(f32[128,8]{1,0:T(8,128)S(1)} %get-tuple-element.18), channel_id=1, replica_groups=mesh['dp'=16,'expert'=16] {'dp'}, use_global_device_ids=true, to_apply=%region_10.11 | all-reduce | flops 1024 | bytes 8192 | tf_op jit(solution)/shard_map/psum | solution.py:182
  540.5 0.7 copy.66
  541.2 4.5 convolution_convert_fusion.4
  545.7 2.2 convolution_convert_fusion.5
  547.9 1.3 copy.62
  549.2 3.9 gather_fusion.4
  553.2 1.0 bitcast_reduce_fusion
  (48 shorter events, 1.1 us)
Async XLA Ops:
  7.2 124.3 %copy-start = (bf16[4,768,256]{2,1,0:T(8,128)(2,1)S(1)}, bf16[4,768,256]{2,1,0:T(8,128)(2,1)}, u32[]{:S(2)}) copy-start(bf16[4,768,256]{2,1,0:T(8,128)(2,1)} %param.12) | copy-start | bytes 4718596
  7.2 267.6 %all-reduce.3.cloned.1.call-start = ((), (), s32[]{:S(2)}) async-start(), calls=%async_computation.8 | async-start | bytes 12582912 | tf_op jit(solution)/shard_map/psum | solution.py:69
  32.4 8.7 %copy-start.2 = (bf16[128,256]{1,0:T(8,128)(2,1)S(1)}, bf16[128,256]{1,0:T(8,128)(2,1)}, u32[]{:S(2)}) copy-start(bf16[128,256]{1,0:T(8,128)(2,1)} %param.7) | copy-start | bytes 196612
  48.6 36.3 %copy-start.9 = (bf16[4,256,768]{2,1,0:T(8,128)(2,1)S(1)}, bf16[4,256,768]{2,1,0:T(8,128)(2,1)}, u32[]{:S(2)}) copy-start(bf16[4,256,768]{2,1,0:T(8,128)(2,1)} %param.11) | copy-start | bytes 4718596
  84.8 5.3 copy-start.3
  84.8 2.7 copy-start.8
  90.2 0.8 copy-start.1
  90.2 271.9 %reduce-scatter.2.cloned.1.call-start = ((), (), s32[]{:S(2)}) async-start(), calls=%async_computation.6 | async-start | bytes 3342336 | tf_op jit(solution)/shard_map/reduce_scatter | solution.py:83
  134.2 311.2 %all-gather.2.cloned.1.call-start = ((), (), s32[]{:S(2)}) async-start(), calls=%async_computation.7 | async-start | bytes 3342336 | tf_op jit(solution)/shard_map/all_gather | solution.py:92
  274.7 5.2 copy-start.5
  366.2 48.1 %all-to-all-start.3 = ((bf16[16,128,768]{2,1,0:T(8,128)(2,1)}), bf16[16,128,768]{2,1,0:T(8,128)(2,1)}, u32[]{:S(2)}, u32[]{:S(2)}) async-start(bf16[16,128,768]{2,1,0:T(8,128)(2,1)} %stack.2), calls=%async_computation.4 | async-start | bytes 6291456 | tf_op jit(solution)/shard_map/all_to_all | solution.py:10
  374.5 1.6 copy-start.7
  414.3 38.5 %all-to-all-start.1 = ((bf16[4,16,32,256]{3,2,0,1:T(8,128)(2,1)}), bf16[4,16,32,256]{3,2,0,1:T(8,128)(2,1)}, u32[]{:S(2)}, u32[]{:S(2)}) async-start(bf16[4,16,32,256]{3,2,0,1:T(8,128)(2,1)} %copy.55), calls=%async_computation.1 | async-start | bytes 2097152 | tf_op jit(solution)/shard_map/all_to_all | solution.py:166
  445.3 3.5 copy-start.10
  452.8 95.1 %all-to-all-start.4 = ((bf16[4,16,32,256]{3,2,0,1:T(8,128)(2,1)}), bf16[4,16,32,256]{3,2,0,1:T(8,128)(2,1)}, u32[]{:S(2)}, u32[]{:S(2)}) async-start(bf16[4,16,32,256]{3,2,0,1:T(8,128)(2,1)} %copy.61), calls=%async_computation.5 | async-start | bytes 2097152 | tf_op jit(solution)/shard_map/all_to_all | solution.py:167
  472.8 73.0 %copy-start.4 = (bf16[4,16,32,256]{3,2,1,0:T(8,128)(2,1)S(1)}, bf16[4,16,32,256]{3,2,1,0:T(8,128)(2,1)}, u32[]{:S(2)}) copy-start(bf16[4,16,32,256]{3,2,1,0:T(8,128)(2,1)} %copy-done.3) | copy-start | bytes 3145732
  541.2 4.5 copy-start.6
Sparse Core Ops, SparseCore 0:
  90.3 184.3 all-reduce.2
  279.1 83.0 reduce-scatter.1
  365.4 79.9 all-gather.1
